TPU v7x, 128 devices: a whole 4x4x4 slice. The times are simulated.
128 devices in a mesh: dp: 32 (over y, z, core), tensor: 4 (over x).
Axes of the slice: x: 4, y: 4, z: 4, core: 2. Of those that a mesh axis runs over, the one named last changes fastest.
Arguments:
- tokens: bfloat16 [16384, 4096], P('dp', 'tensor'), may hold values from -6 to 6
- grad_out: bfloat16 [16384, 4096], P('dp'), may hold values from -3 to 3
- gate_pre: bfloat16 [16384, 14336], P('dp', 'tensor'), may hold values from -9 to 9
- up_value: bfloat16 [16384, 14336], P('dp', 'tensor'), may hold values from -6 to 6
- down_weight: bfloat16 [14336, 4096], P('tensor', 'dp'), may hold values from -0.09375 to 0.09375
- in_proj: bfloat16 [128, 4096], P(None, 'tensor'), may hold values from -0.09375 to 0.09375
- out_proj: bfloat16 [128, 14336], P(None, 'tensor'), may hold values from -0.046875 to 0.046875
- test_matrix: bfloat16 [16384, 128], replicated, may hold values from -0.046875 to 0.046875
Outputs:
- factor: float32 [16384, 128], P(('dp', 'tensor'))
All inputs are finite; a program needn't handle non-finite values.
Results may differ from a plain program's by a relative error of at most 0.0065.
The roundings to bfloat16 on the way count: a program that leaves them out, or rounds other values in their place, can miss the bound.
Values may be sent and summed in bfloat16 or wider, within the bound.
A program may use at most 128 MiB of HBM per device.

v0:
```python
import jax
import jax.numpy as jnp
from jax import lax
from jax.sharding import PartitionSpec as P

SEQ_LEN = 128
shift_scale = 0.1
tiny_value = 1e-06


def local(tokens, grad_out, gate_pre, up_value, down_weight, in_proj, out_proj, test_matrix):
    rows = grad_out.shape[0]
    hidden_grad = lax.dot_general(
        grad_out,
        lax.all_gather(down_weight, "dp", axis=1, tiled=True),
        (((1,), (1,)), ((), ())),
        preferred_element_type=jnp.float32,
    )
    gate_wide = gate_pre.astype(jnp.float32)
    logistic = jax.nn.sigmoid(gate_wide)
    gate_grad = (
        hidden_grad * up_value.astype(jnp.float32) * logistic * (1.0 + gate_wide * (1.0 - logistic))
    ).astype(jnp.bfloat16)
    act_part = lax.dot_general(
        tokens, in_proj, (((1,), (1,)), ((), ())), preferred_element_type=jnp.float32
    )
    out_part = lax.dot_general(
        gate_grad, out_proj, (((1,), (1,)), ((), ())), preferred_element_type=jnp.float32
    )
    act_sum, out_sum = lax.psum((act_part, out_part), "tensor")
    pdim = in_proj.shape[0]
    rank_cols = test_matrix.shape[1]
    seqs_here = rows // SEQ_LEN
    act_seq = act_sum.astype(jnp.bfloat16).reshape(seqs_here, SEQ_LEN, pdim)
    out_seq = out_sum.astype(jnp.bfloat16).reshape(seqs_here, SEQ_LEN, pdim)
    proj_grad = (
        jnp.einsum("slp,slq->spq", act_seq, out_seq, preferred_element_type=jnp.float32)
        .astype(jnp.bfloat16)
        .reshape(seqs_here, pdim * pdim)
    )
    coeff = jnp.dot(proj_grad, test_matrix, preferred_element_type=jnp.float32).astype(jnp.bfloat16)
    dp_count = lax.axis_size("dp")
    tp_count = lax.axis_size("tensor")
    tp_index = lax.axis_index("tensor")
    dp_index = lax.axis_index("dp")
    width = pdim * pdim // (dp_count * tp_count)
    picked = lax.dynamic_slice_in_dim(
        proj_grad.reshape(seqs_here, dp_count, tp_count, width), tp_index, 1, 2
    ).reshape(seqs_here, dp_count * width)
    omega_wide = test_matrix.astype(jnp.float32)
    omega_picked = lax.dynamic_slice_in_dim(
        omega_wide.reshape(dp_count, tp_count, width, rank_cols), tp_index, 1, 1
    ).reshape(dp_count * width, rank_cols)
    omega_own = lax.dynamic_slice_in_dim(omega_picked, dp_index * width, width, 0)
    sketch_part = lax.dot_general(
        picked, coeff, (((0,), (0,)), ((), ())), preferred_element_type=jnp.float32
    )
    gram = lax.dot_general(
        test_matrix, test_matrix, (((0,), (0,)), ((), ())), preferred_element_type=jnp.float32
    )
    omega_sq = jnp.trace(gram)
    summed = lax.psum(sketch_part, "dp")
    core_local = lax.dot_general(
        omega_picked, summed, (((0,), (0,)), ((), ())), precision=lax.Precision.HIGHEST
    )
    square_sum, core_sketch = lax.psum((jnp.sum(summed * summed), core_local), "tensor")
    own_rows = lax.dynamic_slice_in_dim(summed, dp_index * width, width, 0)
    shift = shift_scale * jnp.sqrt(square_sum / (omega_sq + tiny_value))
    core = core_sketch + shift * gram
    core = 0.5 * (core + core.T)
    lower = jnp.linalg.cholesky(core)
    shifted = own_rows + shift * omega_own
    factor = jax.scipy.linalg.solve_triangular(lower, shifted.T, lower=True).T
    return factor


def solution(mesh):
    in_specs = (
        P("dp", "tensor"),
        P("dp", None),
        P("dp", "tensor"),
        P("dp", "tensor"),
        P("tensor", "dp"),
        P(None, "tensor"),
        P(None, "tensor"),
        P(),
    )
    out_specs = P(("dp", "tensor"), None)
    return jax.shard_map(local, mesh=mesh, in_specs=in_specs, out_specs=out_specs, check_vma=False)
```

profile of v0, /device:TPU:0, one launch (start us, length us, event | category | flops | bytes accessed | tf_op | source)
XLA Modules:
  0.0 362.2 jit_solution(9847140538251873871)
XLA Ops:
  6.5 0.7 all-gather.2.cloned.1.call-update
  7.3 0.5 copy-done
  7.8 1.4 fusion.24
  9.1 116.3 %all-gather.2.cloned.1.call-done = bf16[3584,4096]{1,0:T(8,128)(2,1)} async-done(((bf16[3584,128]{1,0:T(8,128)(2,1)}), bf16[3584,4096]{1,0:T(8,128)(2,1)}) %all-gather.2.cloned.1.call-update) | async-done | bytes 29360144 | tf_op jit(solution)/shard_map/all_gather | solution.py:15
  125.4 24.7 %fusion.25 = f32[512,128]{1,0:T(8,128)S(1)} fusion(bf16[128,3584]{1,0:T(8,128)(2,1)} %param.14, bf16[512,3584]{1,0:T(8,128)(2,1)} %param.10, bf16[512,3584]{1,0:T(8,128)(2,1)} %param.11, bf16[512,4096]{1,0:T(8,128)(2,1)} %param.9, bf16[3584,4096]{1,0:T(8,128)(2,1)} %all-gather.2.cloned.1.call-done), kind=kOutput, calls=%fused_computation.40 | convolution fusion | flops 15524167680 | bytes 42074112 | tf_op jit(solution)/shard_map/dot_general | solution.py:27
  150.1 23.1 %all-reduce.8 = (bf16[512,128]{1,0:T(8,128)(2,1)S(1)}, bf16[512,128]{1,0:T(8,128)(2,1)S(1)}) all-reduce(f32[512,128]{1,0:T(8,128)S(1)} %fusion.24, f32[512,128]{1,0:T(8,128)S(1)} %fusion.25), channel_id=1, replica_groups=mesh['dp'=32,'tensor'=4] {'tensor'}, use_global_device_ids=true, to_apply=%region_0.0 | all-reduce | flops 131072 | bytes 786432 | tf_op jit(solution)/shard_map/psum | solution.py:30
  173.2 0.2 convolution_convert_fusion
  173.6 4.7 %fusion.6 = f32[4096,128]{0,1:T(8,128)} fusion(bf16[16384,128]{1,0:T(8,128)(2,1)} %param.15, bf16[1,4,128,128]{3,2,1,0:T(8,128)(2,1)S(1)} %bitcast.60, bf16[1,4,32,128]{3,2,1,0:T(8,128)(2,1)S(1)} %bitcast.61), kind=kOutput, calls=%fused_computation.12 | convolution fusion | flops 20972032 | bytes 6455296 | tf_op jit(solution)/shard_map/dot_general | solution.py:55
  178.6 5.4 %select_reduce_fusion.1 = (f32[]{:T(128)}, f32[128,128]{1,0:T(8,128)S(1)}) fusion(bf16[16384,128]{1,0:T(8,128)(2,1)} %param.15), kind=kOutput, calls=%fused_computation.29 | convolution fusion | flops 536920064 | bytes 4259844 | tf_op jit(solution)/shard_map/dot_general | solution.py:58
  184.0 1.3 constant_dynamic-slice_fusion
  185.3 1.0 copy.28
  186.3 0.3 reshape.38
  186.6 2.9 copy.42
  189.5 96.2 %all-reduce.5.cloned.1.call-done = f32[4096,128]{0,1:T(8,128)} async-done(((f32[4096,128]{0,1:T(8,128)}), f32[4096,128]{0,1:T(8,128)}) %all-reduce.5.cloned.1.call-update) | async-done | bytes 2097168 | tf_op jit(solution)/shard_map/psum | solution.py:62
  285.7 3.3 fusion.26
  289.1 2.7 multiply_reduce_fusion
  292.4 10.9 %psum.38 = f32[]{:T(128)} all-reduce(f32[]{:T(128)} %multiply_reduce_fusion), channel_id=1, replica_groups=mesh['dp'=32,'tensor'=4] {'tensor'}, use_global_device_ids=true, to_apply=%region_4.5 | all-reduce | flops 1 | bytes 8 | tf_op jit(solution)/shard_map/psum | solution.py:66
  303.9 26.1 %all-reduce.7.cloned.1.call-done = f32[128,128]{0,1:T(8,128)} async-done(((f32[128,128]{0,1:T(8,128)}), f32[128,128]{0,1:T(8,128)}) %all-reduce.7.cloned.1.call-update) | async-done | bytes 65552 | tf_op jit(solution)/shard_map/psum | solution.py:66
  330.0 0.8 multiply_add_fusion
  331.0 11.7 %cholesky.13 = f32[128,128]{1,0:T(8,128)S(1)} custom-call(f32[128,128]{1,0:T(8,128)S(1)} %fusion.14), custom_call_target="Cholesky" | custom-call | tf_op jit(solution)/shard_map/jit(cholesky)/cholesky | solution.py:71
  342.8 0.6 compare_reduce_fusion
  343.4 0.7 fusion.11
  344.1 9.8 %custom-call.7 = f32[1,128,128]{1,2,0:T(8,128)S(1)} custom-call(f32[1,128,128]{2,1,0:T(8,128)S(1)} %fusion.11), custom_call_target="InvertDiagBlocksLowerTriangular" | custom-call | tf_op jit(solution)/shard_map/jit(_solve_triangular)/triangular_solve | solution.py:73
  353.9 1.8 fusion.12
  (13 shorter events, 0.8 us)
Async XLA Ops:
  6.5 1.2 copy-start
  6.5 118.9 %all-gather.2.cloned.1.call-start = ((), (), s32[]{:S(2)}) async-start(), calls=%async_computation | async-start | bytes 30277632 | tf_op jit(solution)/shard_map/all_gather | solution.py:15
  7.3 278.4 %all-reduce.5.cloned.1.call-start = ((), (), s32[]{:S(2)}) async-start(), calls=%async_computation.1 | async-start | bytes 4194304 | tf_op jit(solution)/shard_map/psum | solution.py:62
  178.3 151.6 %all-reduce.7.cloned.1.call-start = ((), (), s32[]{:S(2)}) async-start(), calls=%async_computation.2 | async-start | bytes 131072 | tf_op jit(solution)/shard_map/psum | solution.py:66
Sparse Core Ops, SparseCore 0:
  9.5 115.8 all-gather.1
  178.4 107.2 all-reduce.4
  289.2 40.7 all-reduce.6
where the time goes:
time: 363 us; the launch traced here: 362 us
  waiting for transfers between devices  239 us (66%)
  matrix products  41.5 us (11%)
  blocking collectives  34 us (9%)
  other arithmetic  26.7 us (7%)
  between operations  14.4 us (4%)
  local copies, waits for them, and re-layouts  6.14 us (2%)
    all_gather x1, waiting for transfers between devices, local(): lax.all_gather(down_weight, 'dp', axis=1, tiled=True)  116 us
    psum x1, waiting for transfers between devices, local(): summed = lax.psum(sketch_part, 'dp')  96.2 us
    psum x1, waiting for transfers between devices, local(): lax.psum((jnp.sum(summed * summed), core_local), 'tensor')  26.1 us
    dot_general x1, matrix products, local(): lax.dot_general(gate_grad, out_proj, (((1,), (1,)), ((), ())), preferred_...  24.7 us
    psum x1, blocking collectives, local(): act_sum, out_sum = lax.psum((act_part, out_part), 'tensor')  23.1 us
    another operation x3, other arithmetic, local(): lower = jnp.linalg.cholesky(core)  12.4 us
    psum x1, blocking collectives, local(): lax.psum((jnp.sum(summed * summed), core_local), 'tensor')  10.9 us
    another operation x2, other arithmetic, local(): factor = jax.scipy.linalg.solve_triangular(lower, shifted.T, lower=True).T  10.5 us
  transfers between devices with their start and end apart: 3, of which 3 were waited for; matrix products, arithmetic and copies ran while one was open for 4% of the time, Pallas kernels for 0%

commit v1 on v0

--- a/solution.py
+++ b/solution.py
@@ -8,11 +8,16 @@
 tiny_value = 1e-06
 
 
+def all_by_exchange(x, name, dim):
+    sent = jnp.stack([x] * lax.axis_size(name))
+    return jnp.concatenate(lax.all_to_all(sent, name, 0, 0), axis=dim)
+
+
 def local(tokens, grad_out, gate_pre, up_value, down_weight, in_proj, out_proj, test_matrix):
     rows = grad_out.shape[0]
     hidden_grad = lax.dot_general(
         grad_out,
-        lax.all_gather(down_weight, "dp", axis=1, tiled=True),
+        all_by_exchange(down_weight, "dp", 1),
         (((1,), (1,)), ((), ())),
         preferred_element_type=jnp.float32,
     )

time: 363 us -> 744 us (2.05)
  waiting for transfers between devices: 239 us -> 601 us
  local copies, waits for them, and re-layouts: 6.14 us -> 17.3 us
  starting transfers between devices: 0.26 us -> 8.95 us
    all_to_all x0 -> x1, waiting for transfers between devices: none -> 424 us  [all_by_exchange(): return jnp.concatenate(lax.all_to_all(sent, name, 0, 0), axis=dim)]
    all_gather x1 -> x0, waiting for transfers between devices: 116 us -> none  [local(): lax.all_gather(down_weight, 'dp', axis=1, tiled=True)]
    psum x1, waiting for transfers between devices: 96.2 us -> 151 us  [local(): summed = lax.psum(sketch_part, 'dp')]
    another operation x0 -> x1, local copies, waits for them, and re-layouts: none -> 10 us  [all_by_exchange(): sent = jnp.stack([x] * lax.axis_size(name))]
    all_to_all x0 -> x1, starting transfers between devices: none -> 8.69 us  [all_by_exchange(): return jnp.concatenate(lax.all_to_all(sent, name, 0, 0), axis=dim)]
  transfers between devices with their start and end apart: 3 -> 3, of which waited for: 3 -> 3; matrix products, arithmetic and copies ran while one was open for 4% -> 2% of each run, Pallas kernels for 0% -> 0%
where the time goes in v1:
time: 744 us
  waiting for transfers between devices  601 us (81%)
  matrix products  40.8 us (5%)
  blocking collectives  33.8 us (5%)
  other arithmetic  26.7 us (4%)
  local copies, waits for them, and re-layouts  17.3 us (2%)
  between operations  14.8 us (2%)
  starting transfers between devices  8.95 us (1%)
    all_to_all x1, waiting for transfers between devices, all_by_exchange(): return jnp.concatenate(lax.all_to_all(sent, name, 0, 0), axis=dim)  424 us
    psum x1, waiting for transfers between devices, local(): summed = lax.psum(sketch_part, 'dp')  151 us
    psum x1, waiting for transfers between devices, local(): lax.psum((jnp.sum(summed * summed), core_local), 'tensor')  26.5 us
    dot_general x1, matrix products, local(): lax.dot_general(gate_grad, out_proj, (((1,), (1,)), ((), ())), preferred_...  24.9 us
    psum x1, blocking collectives, local(): act_sum, out_sum = lax.psum((act_part, out_part), 'tensor')  22.8 us
  transfers between devices with their start and end apart: 3, of which 3 were waited for; matrix products, arithmetic and copies ran while one was open for 2% of the time, Pallas kernels for 0%

profile of v1, /device:TPU:0, one launch (start us, length us, event | category | flops | bytes accessed | tf_op | source)
XLA Modules:
  0.0 743.5 jit_solution(12576143959404909178)
XLA Ops:
  6.5 1.5 copy.16
  8.1 10.0 %stack.2 = bf16[32,3584,128]{1,2,0:T(8,128)(2,1)} broadcast(bf16[3584,128]{0,1:T(8,128)(2,1)S(1)} %copy.16), dimensions={1,2} | broadcast | bytes 30277632 | tf_op jit(solution)/shard_map/stack | solution.py:12
  18.1 8.7 %all-to-all-start = ((bf16[32,3584,128]{1,2,0:T(8,128)(2,1)}), bf16[32,3584,128]{1,2,0:T(8,128)(2,1)}, u32[]{:S(2)}, u32[]{:S(2)}) async-start(bf16[32,3584,128]{1,2,0:T(8,128)(2,1)} %stack.2), calls=%async_computation | async-start | bytes 58720256 | tf_op jit(solution)/shard_map/all_to_all | solution.py:13
  26.9 0.4 fusion.26
  27.3 424.1 %all-to-all-done = bf16[32,3584,128]{1,2,0:T(8,128)(2,1)} async-done(((bf16[32,3584,128]{1,2,0:T(8,128)(2,1)}), bf16[32,3584,128]{1,2,0:T(8,128)(2,1)}, u32[]{:S(2)}, u32[]{:S(2)}) %all-to-all-start) | async-done | bytes 29360160 | tf_op jit(solution)/shard_map/all_to_all | solution.py:13
  451.4 24.9 %fusion.7 = f32[512,128]{1,0:T(8,128)S(1)} fusion(bf16[128,3584]{1,0:T(8,128)(2,1)S(1)} %copy-done.3, bf16[512,3584]{1,0:T(8,128)(2,1)} %param.10, bf16[512,3584]{1,0:T(8,128)(2,1)} %param.11, bf16[512,4096]{1,0:T(8,128)(2,1)} %param.9, bf16[3584,4096]{0,1:T(8,128)(2,1)} %bitcast.2), kind=kOutput, calls=%fused_computation.13 | convolution fusion | flops 15524167680 | bytes 42074112 | tf_op jit(solution)/shard_map/dot_general | solution.py:32
  476.3 22.8 %all-reduce.8 = (bf16[512,128]{1,0:T(8,128)(2,1)S(1)}, bf16[512,128]{1,0:T(8,128)(2,1)S(1)}) all-reduce(f32[512,128]{1,0:T(8,128)S(1)} %fusion.26, f32[512,128]{1,0:T(8,128)S(1)} %fusion.7), channel_id=1, replica_groups=mesh['dp'=32,'tensor'=4] {'tensor'}, use_global_device_ids=true, to_apply=%region_0.0 | all-reduce | flops 131072 | bytes 786432 | tf_op jit(solution)/shard_map/psum | solution.py:35
  499.6 4.7 fusion.6
  504.5 5.4 select_reduce_fusion.1
  510.0 1.3 constant_dynamic-slice_fusion
  511.3 1.0 copy.29
  512.3 0.3 reshape.48
  512.6 2.9 copy.43
  516.2 150.5 %all-reduce.5.cloned.1.call-done = f32[4096,128]{0,1:T(8,128)} async-done(((f32[4096,128]{0,1:T(8,128)}), f32[4096,128]{0,1:T(8,128)}) %all-reduce.5.cloned.1.call-update) | async-done | bytes 2097168 | tf_op jit(solution)/shard_map/psum | solution.py:67
  666.7 3.3 fusion.27
  670.0 2.7 multiply_reduce_fusion
  672.8 11.0 %psum.38 = f32[]{:T(128)} all-reduce(f32[]{:T(128)} %multiply_reduce_fusion), channel_id=1, replica_groups=mesh['dp'=32,'tensor'=4] {'tensor'}, use_global_device_ids=true, to_apply=%region_4.5 | all-reduce | flops 1 | bytes 8 | tf_op jit(solution)/shard_map/psum | solution.py:71
  684.4 26.5 %all-reduce.7.cloned.1.call-done = f32[128,128]{0,1:T(8,128)} async-done(((f32[128,128]{0,1:T(8,128)}), f32[128,128]{0,1:T(8,128)}) %all-reduce.7.cloned.1.call-update) | async-done | bytes 65552 | tf_op jit(solution)/shard_map/psum | solution.py:71
  710.9 0.8 multiply_add_fusion
  712.0 11.7 %cholesky.13 = f32[128,128]{1,0:T(8,128)S(1)} custom-call(f32[128,128]{1,0:T(8,128)S(1)} %fusion.15), custom_call_target="Cholesky" | custom-call | tf_op jit(solution)/shard_map/jit(cholesky)/cholesky | solution.py:76
  723.8 0.6 compare_reduce_fusion
  724.4 0.7 fusion.12
  725.1 9.8 %custom-call.7 = f32[1,128,128]{1,2,0:T(8,128)S(1)} custom-call(f32[1,128,128]{2,1,0:T(8,128)S(1)} %fusion.12), custom_call_target="InvertDiagBlocksLowerTriangular" | custom-call | tf_op jit(solution)/shard_map/jit(_solve_triangular)/triangular_solve | solution.py:78
  734.9 1.8 fusion.13
  (20 shorter events, 1.1 us)
Async XLA Ops:
  6.5 20.3 %copy-start = (bf16[512,1024]{1,0:T(8,128)(2,1)S(1)}, bf16[512,1024]{1,0:T(8,128)(2,1)}, u32[]{:S(2)}) copy-start(bf16[512,1024]{1,0:T(8,128)(2,1)} %param.8) | copy-start | bytes 3145732
  18.1 8.8 %copy-start.2 = (bf16[128,1024]{1,0:T(8,128)(2,1)S(1)}, bf16[128,1024]{1,0:T(8,128)(2,1)}, u32[]{:S(2)}) copy-start(bf16[128,1024]{1,0:T(8,128)(2,1)} %param.13) | copy-start | bytes 786436
  18.1 433.3 %copy-start.3 = (bf16[128,3584]{1,0:T(8,128)(2,1)S(1)}, bf16[128,3584]{1,0:T(8,128)(2,1)}, u32[]{:S(2)}) copy-start(bf16[128,3584]{1,0:T(8,128)(2,1)} %param.14) | copy-start | bytes 2752516
  18.1 433.3 %all-to-all-start = ((bf16[32,3584,128]{1,2,0:T(8,128)(2,1)}), bf16[32,3584,128]{1,2,0:T(8,128)(2,1)}, u32[]{:S(2)}, u32[]{:S(2)}) async-start(bf16[32,3584,128]{1,2,0:T(8,128)(2,1)} %stack.2), calls=%async_computation | async-start | bytes 58720256 | tf_op jit(solution)/shard_map/all_to_all | solution.py:13
  26.8 639.9 %all-reduce.5.cloned.1.call-start = ((), (), s32[]{:S(2)}) async-start(), calls=%async_computation.1 | async-start | bytes 4194304 | tf_op jit(solution)/shard_map/psum | solution.py:67
  504.3 206.6 %all-reduce.7.cloned.1.call-start = ((), (), s32[]{:S(2)}) async-start(), calls=%async_computation.2 | async-start | bytes 131072 | tf_op jit(solution)/shard_map/psum | solution.py:71
  512.6 224.1 %copy-start.1 = (bf16[512,1024]{1,0:T(8,128)(2,1)S(1)}, bf16[512,1024]{1,0:T(8,128)(2,1)}, u32[]{:S(2)}) copy-start(bf16[512,1024]{1,0:T(8,128)(2,1)} %param.8) | copy-start | bytes 3145732
Sparse Core Ops, SparseCore 0:
  504.4 162.2 all-reduce.4
  670.2 40.7 all-reduce.6

commit v2 on v0

--- a/solution.py
+++ b/solution.py
@@ -59,7 +59,8 @@
         test_matrix, test_matrix, (((0,), (0,)), ((), ())), preferred_element_type=jnp.float32
     )
     omega_sq = jnp.trace(gram)
-    summed = lax.psum(sketch_part, "dp")
+    order_circles = lambda view, mesh_dim: jnp.sum(lax.all_gather(view, mesh_dim), 0)
+    summed = order_circles(sketch_part, "dp")
     core_local = lax.dot_general(
         omega_picked, summed, (((0,), (0,)), ((), ())), precision=lax.Precision.HIGHEST
     )

time: 363 us -> 477 us (1.31)
  waiting for transfers between devices: 239 us -> 334 us
  other arithmetic: 26.7 us -> 46 us
    all_gather x0 -> x1, waiting for transfers between devices: none -> 189 us  [local(): lax.all_gather(view, mesh_dim)]
    psum x1 -> x0, waiting for transfers between devices: 96.2 us -> none  [local(): summed = lax.psum(sketch_part, 'dp')]
    reduce_sum x0 -> x1, other arithmetic: none -> 20.8 us  [local(): jnp.sum(lax.all_gather(view, mesh_dim), 0)]
  transfers between devices with their start and end apart: 3 -> 3, of which waited for: 3 -> 3; matrix products, arithmetic and copies ran while one was open for 4% -> 3% of each run, Pallas kernels for 0% -> 0%
where the time goes in v2:
time: 477 us
  waiting for transfers between devices  334 us (70%)
  other arithmetic  46 us (10%)
  matrix products  41.7 us (9%)
  blocking collectives  34.3 us (7%)
  between operations  14.6 us (3%)
  local copies, waits for them, and re-layouts  6.29 us (1%)
    all_gather x1, waiting for transfers between devices, local(): lax.all_gather(view, mesh_dim)  189 us
    all_gather x1, waiting for transfers between devices, local(): lax.all_gather(down_weight, 'dp', axis=1, tiled=True)  116 us
    psum x1, waiting for transfers between devices, local(): lax.psum((jnp.sum(summed * summed), core_local), 'tensor')  28.1 us
    dot_general x1, matrix products, local(): lax.dot_general(gate_grad, out_proj, (((1,), (1,)), ((), ())), preferred_...  24.7 us
    psum x1, blocking collectives, local(): act_sum, out_sum = lax.psum((act_part, out_part), 'tensor')  23.1 us
    reduce_sum x1, other arithmetic, local(): jnp.sum(lax.all_gather(view, mesh_dim), 0)  20.8 us
    another operation x3, other arithmetic, local(): lower = jnp.linalg.cholesky(core)  12.4 us
    psum x1, blocking collectives, local(): lax.psum((jnp.sum(summed * summed), core_local), 'tensor')  11.2 us
  transfers between devices with their start and end apart: 3, of which 3 were waited for; matrix products, arithmetic and copies ran while one was open for 3% of the time, Pallas kernels for 0%

profile of v2, /device:TPU:0, one launch (start us, length us, event | category | flops | bytes accessed | tf_op | source)
XLA Modules:
  0.0 477.0 jit_solution(5471397343523482794)
XLA Ops:
  6.5 0.7 all-gather.4.cloned.1.call-update
  7.3 0.5 copy-done
  7.8 1.4 fusion.23
  9.1 116.3 %all-gather.4.cloned.1.call-done = bf16[3584,4096]{1,0:T(8,128)(2,1)} async-done(((bf16[3584,128]{1,0:T(8,128)(2,1)}), bf16[3584,4096]{1,0:T(8,128)(2,1)}) %all-gather.4.cloned.1.call-update) | async-done | bytes 29360144 | tf_op jit(solution)/shard_map/all_gather | solution.py:15
  125.4 24.7 %fusion.24 = f32[512,128]{1,0:T(8,128)S(1)} fusion(bf16[128,3584]{1,0:T(8,128)(2,1)} %param.14, bf16[512,3584]{1,0:T(8,128)(2,1)} %param.10, bf16[512,3584]{1,0:T(8,128)(2,1)} %param.11, bf16[512,4096]{1,0:T(8,128)(2,1)} %param.9, bf16[3584,4096]{1,0:T(8,128)(2,1)} %all-gather.4.cloned.1.call-done), kind=kOutput, calls=%fused_computation.40 | convolution fusion | flops 15524167680 | bytes 42074112 | tf_op jit(solution)/shard_map/dot_general | solution.py:27
  150.1 23.1 %all-reduce.5 = (bf16[512,128]{1,0:T(8,128)(2,1)S(1)}, bf16[512,128]{1,0:T(8,128)(2,1)S(1)}) all-reduce(f32[512,128]{1,0:T(8,128)S(1)} %fusion.23, f32[512,128]{1,0:T(8,128)S(1)} %fusion.24), channel_id=1, replica_groups=mesh['dp'=32,'tensor'=4] {'tensor'}, use_global_device_ids=true, to_apply=%region_0.0 | all-reduce | flops 131072 | bytes 786432 | tf_op jit(solution)/shard_map/psum | solution.py:30
  173.6 4.6 fusion.6
  178.5 5.4 %select_reduce_fusion.1 = (f32[]{:T(128)}, f32[128,128]{1,0:T(8,128)S(1)}) fusion(bf16[16384,128]{1,0:T(8,128)(2,1)} %param.15), kind=kOutput, calls=%fused_computation.29 | convolution fusion | flops 536920064 | bytes 4259844 | tf_op jit(solution)/shard_map/dot_general | solution.py:58
  184.0 1.3 constant_dynamic-slice_fusion
  185.3 1.0 copy.34
  186.3 0.3 reshape.38
  186.6 3.0 copy.48
  190.2 188.8 %all-gather.6.cloned.1.call-done = f32[131072,128]{1,0:T(8,128)} async-done(((f32[4096,128]{1,0:T(8,128)}), f32[131072,128]{1,0:T(8,128)}) %all-gather.6.cloned.1.call-update) | async-done | bytes 67108880 | tf_op jit(solution)/shard_map/all_gather | solution.py:62
  379.0 20.8 %reduce_sum.28 = f32[4096,128]{1,0:T(8,128)S(1)} reduce(f32[32,4096,128]{2,1,0:T(8,128)} %bitcast.3, f32[]{:T(128)} %constant.62.clone.1), dimensions={0}, to_apply=%region_2.3 | reduce | flops 16252928 | bytes 69206016 | tf_op jit(solution)/shard_map/reduce_sum | solution.py:62
  399.8 1.2 multiply_reduce_fusion
  401.0 3.7 fusion.25
  404.7 11.2 %psum.30 = f32[]{:T(128)} all-reduce(f32[]{:T(128)} %multiply_reduce_fusion), channel_id=1, replica_groups=mesh['dp'=32,'tensor'=4] {'tensor'}, use_global_device_ids=true, to_apply=%region_4.5 | all-reduce | flops 1 | bytes 8 | tf_op jit(solution)/shard_map/psum | solution.py:67
  416.7 28.1 %all-reduce.4.cloned.1.call-done = f32[128,128]{0,1:T(8,128)} async-done(((f32[128,128]{0,1:T(8,128)}), f32[128,128]{0,1:T(8,128)}) %all-reduce.4.cloned.1.call-update) | async-done | bytes 65552 | tf_op jit(solution)/shard_map/psum | solution.py:67
  444.8 0.8 multiply_add_fusion
  445.9 11.7 %cholesky.13 = f32[128,128]{1,0:T(8,128)S(1)} custom-call(f32[128,128]{1,0:T(8,128)S(1)} %fusion.14), custom_call_target="Cholesky" | custom-call | tf_op jit(solution)/shard_map/jit(cholesky)/cholesky | solution.py:72
  457.6 0.6 compare_reduce_fusion
  458.3 0.7 fusion.11
  458.9 9.8 %custom-call.7 = f32[1,128,128]{1,2,0:T(8,128)S(1)} custom-call(f32[1,128,128]{2,1,0:T(8,128)S(1)} %fusion.11), custom_call_target="InvertDiagBlocksLowerTriangular" | custom-call | tf_op jit(solution)/shard_map/jit(_solve_triangular)/triangular_solve | solution.py:74
  468.7 1.8 fusion.12
  (18 shorter events, 1.2 us)
Async XLA Ops:
  6.5 1.2 copy-start
  6.5 118.9 %all-gather.4.cloned.1.call-start = ((), (), s32[]{:S(2)}) async-start(), calls=%async_computation | async-start | bytes 30277632 | tf_op jit(solution)/shard_map/all_gather | solution.py:15
  7.3 371.7 %all-gather.6.cloned.1.call-start = ((), (), s32[]{:S(2)}) async-start(), calls=%async_computation.2 | async-start | bytes 69206016 | tf_op jit(solution)/shard_map/all_gather | solution.py:62
  178.3 266.5 %all-reduce.4.cloned.1.call-start = ((), (), s32[]{:S(2)}) async-start(), calls=%async_computation.1 | async-start | bytes 131072 | tf_op jit(solution)/shard_map/psum | solution.py:67
  185.3 4.2 copy-start.1
Sparse Core Ops, SparseCore 0:
  9.5 115.8 all-gather.3
  178.4 200.5 all-gather.5
  404.8 39.9 all-reduce.3
